TPU v7x, 32 devices: a whole 2x2x4 slice. The times are simulated.
32 devices in a mesh: req: 16 (over z, y, x), mlp: 2 (over core).
Axes of the slice: x: 2, y: 2, z: 4, core: 2. Of those that a mesh axis runs over, the one named last changes fastest.
Arguments:
- queries: bfloat16 [16, 256, 1536], P('req'), may hold values from -90 to 90
- cached_key_slots: bfloat16 [16, 8192, 512], P('req', 'mlp'), may hold values from -5 to 5
- cached_value_slots: bfloat16 [16, 8192, 512], P('req', 'mlp'), may hold values from -6 to 6
- new_token_keys: bfloat16 [16, 256, 512], P('req', 'mlp'), may hold values from -5.05 to 5.05
- new_token_values: bfloat16 [16, 256, 512], P('req', 'mlp'), may hold values from -6 to 6
- cache_len: int32 [16], replicated, may hold values from 1 to 8192, 65536 in all
- placing: int32 [16], replicated, may hold values from 0 to 15, each once
- w_gate: bfloat16 [1536, 12288], P('req', 'mlp'), may hold values from -0.15625 to 0.15625
- w_up: bfloat16 [1536, 12288], P('req', 'mlp'), may hold values from -0.15625 to 0.15625
- w_down: bfloat16 [12288, 1536], P('mlp', 'req'), may hold values from -0.0546875 to 0.0546875
Outputs:
- mixed: bfloat16 [16, 256, 1536], P('req', 'mlp')
All inputs are finite; a program needn't handle non-finite values.
Results may differ from a plain program's by a relative error of at most 0.019.
Values may be sent and summed in bfloat16 or wider, within the bound.
A program may use at most 192 MiB of HBM per device.

v0:
```python
import jax
import jax.numpy as jnp
from jax import lax
from jax.sharding import PartitionSpec as P

HEAD_SIZE = 256
QUERY_HEADS = 6
KEY_VALUE_HEADS = 2
score_scale = 0.0625
negative = -1e30


def lookup(table, index):
    positions = jnp.arange(table.shape[0], dtype=jnp.int32)
    return jnp.sum(jnp.where(positions == index, table, 0))


def rms_rows(attended):
    wide = attended.astype(jnp.float32)
    return (wide * lax.rsqrt(jnp.mean(wide * wide, axis=-1, keepdims=True) + 1e-06)).astype(
        jnp.bfloat16
    )


def gathered_weights(weighted, denom_local, w_gate, w_up, w_down):
    token_inputs = weighted.shape[0]
    mlp_index = lax.axis_index("mlp")
    row_count = token_inputs // lax.axis_size("mlp")
    weighted, denom = lax.psum((weighted, denom_local), "mlp")
    attended = (
        (weighted / jnp.transpose(denom, (2, 0, 1))[..., None])
        .reshape(token_inputs, QUERY_HEADS * HEAD_SIZE)
        .astype(jnp.bfloat16)
    )
    normed = rms_rows(attended)
    own_attended = lax.dynamic_slice_in_dim(attended, mlp_index * row_count, row_count, 0)
    gate_sum = jnp.dot(
        normed,
        lax.all_gather(w_gate, "req", axis=0, tiled=True),
        preferred_element_type=jnp.float32,
    )
    upper_sum = jnp.dot(
        normed, lax.all_gather(w_up, "req", axis=0, tiled=True), preferred_element_type=jnp.float32
    )
    hidden = (jax.nn.silu(gate_sum) * upper_sum).astype(jnp.bfloat16)
    partial_down = jnp.dot(
        hidden,
        lax.all_gather(w_down, "req", axis=1, tiled=True),
        preferred_element_type=jnp.float32,
    )
    own_rows = lax.psum_scatter(
        partial_down.astype(jnp.bfloat16), "mlp", scatter_dimension=0, tiled=True
    ).astype(jnp.float32)
    residual = own_attended.astype(jnp.float32)
    return (residual + own_rows).astype(jnp.bfloat16)[None]


def body(
    queries,
    cached_key_slots,
    cached_value_slots,
    new_token_keys,
    new_token_values,
    cache_len,
    placing,
    w_gate,
    w_up,
    w_down,
):
    slot_index = lax.axis_index("req")
    mlp_index = lax.axis_index("mlp")
    mlp_count = lax.axis_size("mlp")
    token_inputs = queries.shape[1]
    request_cache = cached_key_slots.shape[1]
    request_new_tokens = new_token_keys.shape[1]
    query_group_width = QUERY_HEADS // KEY_VALUE_HEADS
    row_count = token_inputs // mlp_count
    request = lookup(placing, slot_index)
    live_len = lookup(cache_len, request)
    query_head_rows = queries[0].reshape(
        token_inputs, KEY_VALUE_HEADS, query_group_width, HEAD_SIZE
    )
    request_keys = cached_key_slots[0].reshape(request_cache, KEY_VALUE_HEADS, HEAD_SIZE)
    request_values = cached_value_slots[0].reshape(request_cache, KEY_VALUE_HEADS, HEAD_SIZE)
    new_key_rows = new_token_keys[0].reshape(request_new_tokens, KEY_VALUE_HEADS, HEAD_SIZE)
    new_value_rows = new_token_values[0].reshape(request_new_tokens, KEY_VALUE_HEADS, HEAD_SIZE)
    cache_pos = mlp_index * request_cache + jnp.arange(request_cache, dtype=jnp.int32)
    cache_live = cache_pos < live_len
    scores_old = (
        jnp.einsum(
            "ngrd,cgd->grnc", query_head_rows, request_keys, preferred_element_type=jnp.float32
        )
        * score_scale
    )
    scores_old = jnp.where(cache_live[None, None, None, :], scores_old, negative)
    fresh_pos = mlp_index * request_new_tokens + jnp.arange(request_new_tokens, dtype=jnp.int32)
    causal = fresh_pos[None, :] <= jnp.arange(token_inputs, dtype=jnp.int32)[:, None]
    scores_new = (
        jnp.einsum(
            "ngrd,mgd->grnm", query_head_rows, new_key_rows, preferred_element_type=jnp.float32
        )
        * score_scale
    )
    scores_new = jnp.where(causal[None, None], scores_new, negative)
    local_top = jnp.maximum(scores_old.max(-1), scores_new.max(-1))
    row_top = lax.pmax(local_top, "mlp")
    expo_old = jnp.exp(scores_old - row_top[..., None])
    expo_new = jnp.exp(scores_new - row_top[..., None])
    denom_local = expo_old.sum(-1) + expo_new.sum(-1)
    probs_old = expo_old.astype(jnp.bfloat16)
    probs_new = expo_new.astype(jnp.bfloat16)
    weighted = jnp.einsum(
        "grnc,cgd->ngrd", probs_old, request_values, preferred_element_type=jnp.float32
    )
    weighted = weighted + jnp.einsum(
        "grnm,mgd->ngrd", probs_new, new_value_rows, preferred_element_type=jnp.float32
    )
    if lax.axis_size("req") > 16:
        return gathered_weights(weighted, denom_local, w_gate, w_up, w_down)
    w_in = jnp.stack([w_gate, w_up])
    w_in = lax.all_to_all(w_in, "req", split_axis=2, concat_axis=1, tiled=True)
    w_in = lax.all_gather(w_in, "mlp", axis=2, tiled=True)
    w_out = lax.all_to_all(w_down, "req", split_axis=0, concat_axis=1, tiled=True)
    w_out = lax.all_gather(w_out, "mlp", axis=0, tiled=True)
    denom_rows = jnp.transpose(denom_local, (2, 0, 1))
    weighted = lax.psum_scatter(weighted, "mlp", scatter_dimension=0, tiled=True)
    denom = lax.psum_scatter(denom_rows, "mlp", scatter_dimension=0, tiled=True)
    attended = (
        (weighted / denom[..., None])
        .reshape(row_count, QUERY_HEADS * HEAD_SIZE)
        .astype(jnp.bfloat16)
    )
    normed = lax.all_gather(rms_rows(attended), "req", axis=0, tiled=True)
    gate_sum = jnp.dot(normed, w_in[0], preferred_element_type=jnp.float32)
    upper_sum = jnp.dot(normed, w_in[1], preferred_element_type=jnp.float32)
    hidden = (jax.nn.silu(gate_sum) * upper_sum).astype(jnp.bfloat16)
    partial_down = jnp.dot(hidden, w_out, preferred_element_type=jnp.float32)
    own_rows = lax.psum_scatter(
        partial_down.astype(jnp.bfloat16), "req", scatter_dimension=0, tiled=True
    ).astype(jnp.float32)
    return (attended.astype(jnp.float32) + own_rows).astype(jnp.bfloat16)[None]


def solution(mesh):
    in_specs = (
        P("req", None, None),
        P("req", "mlp", None),
        P("req", "mlp", None),
        P("req", "mlp", None),
        P("req", "mlp", None),
        P(),
        P(),
        P("req", "mlp"),
        P("req", "mlp"),
        P("mlp", "req"),
    )
    out_specs = P("req", "mlp", None)
    return jax.shard_map(body, mesh=mesh, in_specs=in_specs, out_specs=out_specs, check_vma=False)
```

profile of v0, /device:TPU:0, one launch (start us, length us, event | category | flops | bytes accessed | tf_op | source)
XLA Modules:
  0.0 450.4 jit_solution(2439042109606651874)
XLA Ops:
  6.5 1.4 copy.59
  8.0 6.9 %reshape_squeeze.15 = bf16[4096,2,256]{2,1,0:T(2,128)(2,1)} reshape(bf16[1,4096,512]{2,1,0:T(8,128)(2,1)} %param.11) | data formatting | bytes 8388608 | tf_op jit(solution)/shard_map/reshape;squeeze | solution.py:83
  15.1 0.6 fusion.20
  15.8 1.3 fusion.21
  17.0 0.6 add_compare_fusion
  17.6 12.0 %bitcast_reduce_fusion = (f32[2,3,256]{2,1,0:T(4,128)S(1)}, f32[2,4096,256,3]{2,1,3,0:T(8,128)}) fusion(pred[4096]{0:T(1024)(128)(4,1)S(1)} %add_compare_fusion, bf16[256,2,3,256]{0,3,2,1:T(8,128)(2,1)S(1)} %bitcast.63, bf16[4096,2,256,1]{2,1,0,3:T(2,128)(2,1)} %bitcast.61), kind=kOutput, calls=%fused_computation.1 | convolution fusion | flops 3240098304 | bytes 30156800 | tf_op jit(solution)/shard_map/ngrd,cgd->grnc/dot_general | solution.py:90
  29.6 0.3 fusion.25
  29.9 2.6 pmax.7
  32.5 11.5 %fusion.1 = f32[2,3,256]{2,1,0:T(4,128)S(1)} fusion(f32[2,4096,256,3]{2,1,3,0:T(8,128)} %get-tuple-element.8, f32[2,3,256]{2,1,0:T(4,128)S(1)} %pmax.7, pred[4096]{0:T(1024)(128)(4,1)S(1)} %add_compare_fusion), kind=kLoop, calls=%fused_computation.4 | loop fusion | flops 25164288 | bytes 25182208 | tf_op jit(solution)/shard_map/reduce_sum | solution.py:109
  44.0 0.1 fusion.12
  44.2 0.8 copy.94
  45.0 1.5 pad_maximum_fusion
  46.5 5.3 %copy.69 = bf16[2,96,6144]{1,0,2:T(2,128)(2,1)} copy(bf16[2,96,6144]{2,1,0:T(8,128)(2,1)S(1)} %pad_maximum_fusion) | data formatting | bytes 4718592 | tf_op jit(solution)/shard_map/stack | solution.py:120
  51.9 8.2 %all-to-all-start = ((bf16[2,96,6144]{1,0,2:T(2,128)(2,1)}), bf16[2,96,6144]{1,0,2:T(2,128)(2,1)S(1)}, u32[]{:S(2)}, u32[]{:S(2)}) async-start(bf16[2,96,6144]{1,0,2:T(2,128)(2,1)} %copy.69), calls=%async_computation.1 | async-start | bytes 6291456 | tf_op jit(solution)/shard_map/all_to_all | solution.py:121
  60.1 6.9 %reshape_squeeze.18 = bf16[4096,2,256]{2,1,0:T(2,128)(2,1)} reshape(bf16[1,4096,512]{2,1,0:T(8,128)(2,1)} %param.12) | data formatting | bytes 8388608 | tf_op jit(solution)/shard_map/reshape;squeeze | solution.py:84
  67.1 13.5 %fusion.3 = f32[2,3,256,256]{3,2,1,0:T(8,128)S(1)} fusion(f32[2,4096,256,3]{2,1,3,0:T(8,128)} %get-tuple-element.8, f32[2,3,256]{2,1,0:T(4,128)S(1)} %pmax.7, pred[4096]{0:T(1024)(128)(4,1)S(1)} %add_compare_fusion, bf16[4096,2,256,1]{2,1,0,3:T(2,128)(2,1)} %bitcast.62), kind=kOutput, calls=%fused_computation.6 | convolution fusion | flops 3246391296 | bytes 30943232 | tf_op jit(solution)/shard_map/grnc,cgd->ngrd/dot_general | solution.py:112
  80.6 1.6 add_bitcast_fusion
  82.3 38.9 %all-to-all-done = bf16[2,96,6144]{1,0,2:T(2,128)(2,1)S(1)} async-done(((bf16[2,96,6144]{1,0,2:T(2,128)(2,1)}), bf16[2,96,6144]{1,0,2:T(2,128)(2,1)S(1)}, u32[]{:S(2)}, u32[]{:S(2)}) %all-to-all-start) | async-done | bytes 2359328 | tf_op jit(solution)/shard_map/all_to_all | solution.py:121
  121.2 5.5 %copy.91 = bf16[2,96,16,384]{3,1,2,0:T(8,128)(2,1)} copy(bf16[2,96,16,384]{1,0,3,2:T(2,128)(2,1)S(1)} %bitcast.56) | data formatting | bytes 4718592 | tf_op jit(solution)/shard_map/all_to_all | solution.py:121
  126.8 1.0 reshape.52
  128.0 1.4 multiply_reduce_fusion
  129.4 0.3 copy.68
  129.7 0.8 multiply_convert_fusion.1
  130.7 44.9 %all_to_all.37 = bf16[16,384,96]{1,2,0:T(8,128)(2,1)} all-to-all(bf16[16,384,96]{1,2,0:T(8,128)(2,1)S(1)} %bitcast.60), channel_id=1, replica_groups=mesh['req'=16,'mlp'=2] {'req'}, dimensions={0} | all-to-all | bytes 2359296 | tf_op jit(solution)/shard_map/all_to_all | solution.py:123
  175.6 0.2 reduce-scatter.8.cloned.1.call-start
  175.9 96.7 %all-gather.4.cloned.1.call-done = bf16[2048,1536]{0,1:T(8,128)(2,1)} async-done(((bf16[128,1536]{0,1:T(8,128)(2,1)}), bf16[2048,1536]{0,1:T(8,128)(2,1)}) %all-gather.4.cloned.1.call-update) | async-done | bytes 6291472 | tf_op jit(solution)/shard_map/all_gather | solution.py:133
  272.6 8.3 %fusion.9 = f32[2048,768]{1,0:T(8,128)S(1)} fusion(bf16[2048,1536]{0,1:T(8,128)(2,1)} %all-gather.4.cloned.1.call-done, bf16[2,1536,768]{2,1,0:T(8,128)(2,1)} %all-gather.6.cloned.1.call-done), kind=kOutput, calls=%fused_computation.15 | convolution fusion | flops 4831838208 | bytes 14942208 | tf_op jit(solution)/shard_map/dot_general | solution.py:134
  280.9 7.6 %multiply_convert_fusion = bf16[2048,768]{1,0:T(8,128)(2,1)} fusion(f32[2048,768]{1,0:T(8,128)S(1)} %fusion.9, bf16[2048,1536]{0,1:T(8,128)(2,1)S(1)} %copy-done.6, bf16[2,1536,768]{2,1,0:T(8,128)(2,1)S(1)} %copy-done.7), kind=kOutput, calls=%fused_computation.9 | convolution fusion | flops 4841275392 | bytes 18087936 | tf_op jit(solution)/shard_map/dot_general | solution.py:135
  288.5 9.1 %convolution_convert_fusion = bf16[2048,1536]{1,0:T(8,128)(2,1)} fusion(bf16[2048,768]{1,0:T(8,128)(2,1)} %multiply_convert_fusion, bf16[768,1536]{0,1:T(8,128)(2,1)} %all-gather.8.cloned.1.call-done), kind=kOutput, calls=%fused_computation.8 | convolution fusion | flops 4834983936 | bytes 11796480 | tf_op jit(solution)/shard_map/dot_general | solution.py:137
  297.7 0.3 copy.73
  298.0 143.7 %reduce-scatter.8.cloned.1.call-done = bf16[128,1536]{1,0:T(8,128)(2,1)} async-done(((bf16[2048,1536]{1,0:T(8,128)(2,1)}), bf16[128,1536]{1,0:T(8,128)(2,1)}) %reduce-scatter.8.cloned.1.call-update) | async-done | bytes 393232 | tf_op jit(solution)/shard_map/reduce_scatter | solution.py:138
  441.7 1.8 fusion.16
  (45 shorter events, 0.7 us)
Async XLA Ops:
  6.5 120.3 %reduce-scatter.10.cloned.1.call-start = ((), (), s32[]{:S(2)}) async-start(), calls=%async_computation.10 | async-start | bytes 196608
  6.5 8.4 %copy-start.4 = (bf16[1,128,512]{2,1,0:T(8,128)(2,1)S(1)}, bf16[1,128,512]{2,1,0:T(8,128)(2,1)}, u32[]{:S(2)}) copy-start(bf16[1,128,512]{2,1,0:T(8,128)(2,1)} %param.13) | copy-start | bytes 393220
  8.0 7.1 %copy-start.8 = (s32[16]{0:T(128)S(1)}, s32[16]{0:T(128)}, u32[]{:S(2)}) copy-start(s32[16]{0:T(128)} %param.16) | copy-start | bytes 196
  8.0 7.8 %copy-start.9 = (s32[16]{0:T(128)S(1)}, s32[16]{0:T(128)}, u32[]{:S(2)}) copy-start(s32[16]{0:T(128)} %param.15) | copy-start | bytes 196
  29.8 14.2 %copy-start = (f32[2,3,256,128]{2,3,1,0:T(8,128)}, f32[2,3,256,128]{2,3,1,0:T(8,128)S(1)}, u32[]{:S(2)}) copy-start(f32[2,3,256,128]{2,3,1,0:T(8,128)S(1)} %get-tuple-element.10) | copy-start | bytes 2359300
  32.5 12.5 %copy-start.3 = (bf16[96,6144]{1,0:T(8,128)(2,1)S(1)}, bf16[96,6144]{1,0:T(8,128)(2,1)}, u32[]{:S(2)}) copy-start(bf16[96,6144]{1,0:T(8,128)(2,1)} %param.18) | copy-start | bytes 3538948
  51.9 69.4 %all-to-all-start = ((bf16[2,96,6144]{1,0,2:T(2,128)(2,1)}), bf16[2,96,6144]{1,0,2:T(2,128)(2,1)S(1)}, u32[]{:S(2)}, u32[]{:S(2)}) async-start(bf16[2,96,6144]{1,0,2:T(2,128)(2,1)} %copy.69), calls=%async_computation.1 | async-start | bytes 6291456 | tf_op jit(solution)/shard_map/all_to_all | solution.py:121
  60.1 7.0 %copy-start.5 = (bf16[1,128,512]{2,1,0:T(8,128)(2,1)S(1)}, bf16[1,128,512]{2,1,0:T(8,128)(2,1)}, u32[]{:S(2)}) copy-start(bf16[1,128,512]{2,1,0:T(8,128)(2,1)} %param.14) | copy-start | bytes 393220
  60.1 67.9 %reduce-scatter.6.cloned.1.call-start = ((), (), s32[]{:S(2)}) async-start(), calls=%async_computation.5 | async-start | bytes 2359296 | tf_op jit(solution)/shard_map/reduce_scatter | solution.py:126
  67.1 13.5 %copy-start.1 = (f32[2,3,256,128]{2,3,1,0:T(8,128)S(1)}, f32[2,3,256,128]{2,3,1,0:T(8,128)}, u32[]{:S(2)}) copy-start(f32[2,3,256,128]{2,3,1,0:T(8,128)} %copy-done) | copy-start | bytes 2359300
  82.3 93.6 %all-gather.6.cloned.1.call-start = ((), (), s32[]{:S(2)}) async-start(), calls=%async_computation.7 | async-start | bytes 7077888 | tf_op jit(solution)/shard_map/all_gather | solution.py:122
  126.7 3.8 copy-start.2
  126.8 145.9 %all-gather.4.cloned.1.call-start = ((), (), s32[]{:S(2)}) async-start(), calls=%async_computation.6 | async-start | bytes 6684672 | tf_op jit(solution)/shard_map/all_gather | solution.py:133
  130.5 158.1 %all-gather.8.cloned.1.call-start = ((), (), s32[]{:S(2)}) async-start(), calls=%async_computation.8 | async-start | bytes 3538944 | tf_op jit(solution)/shard_map/all_gather | solution.py:124
  175.6 266.1 %reduce-scatter.8.cloned.1.call-start = ((), (), s32[]{:S(2)}) async-start(), calls=%async_computation.9 | async-start | bytes 6684672 | tf_op jit(solution)/shard_map/reduce_scatter | solution.py:138
  272.6 8.3 %copy-start.6 = (bf16[2048,1536]{0,1:T(8,128)(2,1)S(1)}, bf16[2048,1536]{0,1:T(8,128)(2,1)}, u32[]{:S(2)}) copy-start(bf16[2048,1536]{0,1:T(8,128)(2,1)} %all-gather.4.cloned.1.call-done) | copy-start | bytes 18874372
  272.6 8.3 %copy-start.7 = (bf16[2,1536,768]{2,1,0:T(8,128)(2,1)S(1)}, bf16[2,1536,768]{2,1,0:T(8,128)(2,1)}, u32[]{:S(2)}) copy-start(bf16[2,1536,768]{2,1,0:T(8,128)(2,1)} %all-gather.6.cloned.1.call-done) | copy-start | bytes 14155780
Sparse Core Ops, SparseCore 0:
  45.1 10.0 reduce-scatter.9
  82.4 10.3 reduce-scatter.5
  126.9 24.3 all-gather.5
  154.2 118.3 all-gather.3
  274.1 9.0 all-gather.7
  297.8 143.8 reduce-scatter.7
where the time goes:
time: 451 us; the launch traced here: 450 us
  waiting for transfers between devices  280 us (62%)
  matrix products  52.4 us (12%)
  blocking collectives  47.6 us (11%)
  local copies, waits for them, and re-layouts  28.9 us (6%)
  other arithmetic  19.7 us (4%)
  between operations  13.7 us (3%)
  starting transfers between devices  8.58 us (2%)
    reduce_scatter x1, waiting for transfers between devices, body(): lax.psum_scatter(partial_down.astype(jnp.bfloat16), 'req', scatter_dimens...  144 us
    all_gather x1, waiting for transfers between devices, body(): normed = lax.all_gather(rms_rows(attended), 'req', axis=0, tiled=True)  96.7 us
    all_to_all x1, blocking collectives, body(): lax.all_to_all(w_down, 'req', split_axis=0, concat_axis=1, tiled=True)  44.9 us
    all_to_all x1, waiting for transfers between devices, body(): w_in = lax.all_to_all(w_in, 'req', split_axis=2, concat_axis=1, tiled=True)  38.9 us
    dot_general x1, matrix products, body(): jnp.einsum('grnc,cgd->ngrd', probs_old, request_values, preferred_element...  13.5 us
    dot_general x1, matrix products, body(): jnp.einsum('ngrd,cgd->grnc', query_head_rows, request_keys, preferred_ele...  12 us
    reduce_sum x2, other arithmetic, body(): denom_local = expo_old.sum(-1) + expo_new.sum(-1)  11.7 us
    dot_general x1, matrix products, body(): partial_down = jnp.dot(hidden, w_out, preferred_element_type=jnp.float32)  9.13 us
  transfers between devices with their start and end apart: 7, of which 3 were waited for; matrix products, arithmetic and copies ran while one was open for 12% of the time, Pallas kernels for 0%

commit v1 on v0

--- a/solution.py
+++ b/solution.py
@@ -118,7 +118,10 @@
     if lax.axis_size("req") > 16:
         return gathered_weights(weighted, denom_local, w_gate, w_up, w_down)
     w_in = jnp.stack([w_gate, w_up])
-    w_in = lax.all_to_all(w_in, "req", split_axis=2, concat_axis=1, tiled=True)
+    w_in = jnp.concatenate(
+        lax.all_to_all(jnp.stack(jnp.split(w_in, lax.axis_size("req"), axis=2)), "req", 0, 0),
+        axis=1,
+    )
     w_in = lax.all_gather(w_in, "mlp", axis=2, tiled=True)
     w_out = lax.all_to_all(w_down, "req", split_axis=0, concat_axis=1, tiled=True)
     w_out = lax.all_gather(w_out, "mlp", axis=0, tiled=True)

time: 451 us -> 434 us (0.962)
  waiting for transfers between devices: 280 us -> 266 us
  other arithmetic: 19.7 us -> 29.4 us
  local copies, waits for them, and re-layouts: 28.9 us -> 19.7 us
    all_to_all x1, waiting for transfers between devices: 38.9 us -> 25.5 us  [body(): lax.all_to_all(jnp.stack(jnp.split(w_in, lax.axis_size('req'), axis=2)),...]
    unnamed x0 -> x15, other arithmetic: none -> 10.1 us
    another operation x1 -> x0, local copies, waits for them, and re-layouts: 5.33 us -> none  [body(): w_in = jnp.stack([w_gate, w_up])]
  transfers between devices with their start and end apart: 7 -> 7, of which waited for: 3 -> 3; matrix products, arithmetic and copies ran while one was open for 12% -> 13% of each run, Pallas kernels for 0% -> 0%
where the time goes in v1:
time: 434 us; the launch traced here: 433 us
  waiting for transfers between devices  266 us (61%)
  matrix products  52.3 us (12%)
  blocking collectives  43.4 us (10%)
  other arithmetic  29.4 us (7%)
  local copies, waits for them, and re-layouts  19.7 us (5%)
  between operations  13.7 us (3%)
  starting transfers between devices  8.59 us (2%)
    reduce_scatter x1, waiting for transfers between devices, body(): lax.psum_scatter(partial_down.astype(jnp.bfloat16), 'req', scatter_dimens...  144 us
    all_gather x1, waiting for transfers between devices, body(): normed = lax.all_gather(rms_rows(attended), 'req', axis=0, tiled=True)  96.8 us
    all_to_all x1, blocking collectives, body(): lax.all_to_all(w_down, 'req', split_axis=0, concat_axis=1, tiled=True)  40.8 us
    all_to_all x1, waiting for transfers between devices, body(): lax.all_to_all(jnp.stack(jnp.split(w_in, lax.axis_size('req'), axis=2)),...  25.5 us
    dot_general x1, matrix products, body(): jnp.einsum('grnc,cgd->ngrd', probs_old, request_values, preferred_element...  13.5 us
    dot_general x1, matrix products, body(): jnp.einsum('ngrd,cgd->grnc', query_head_rows, request_keys, preferred_ele...  12 us
    reduce_sum x2, other arithmetic, body(): denom_local = expo_old.sum(-1) + expo_new.sum(-1)  11.7 us
    unnamed x15, other arithmetic  10.1 us
  transfers between devices with their start and end apart: 7, of which 3 were waited for; matrix products, arithmetic and copies ran while one was open for 13% of the time, Pallas kernels for 0%

profile of v1, /device:TPU:0, one launch (start us, length us, event | category | flops | bytes accessed | tf_op | source)
XLA Modules:
  0.0 433.4 jit_solution(8052339502175823979)
XLA Ops:
  6.5 1.4 copy.72
  8.0 7.0 %reshape_squeeze.15 = bf16[4096,2,256]{2,1,0:T(2,128)(2,1)} reshape(bf16[1,4096,512]{2,1,0:T(8,128)(2,1)} %param.11) | data formatting | bytes 8388608 | tf_op jit(solution)/shard_map/reshape;squeeze | solution.py:83
  15.8 1.4 fusion.38
  17.1 0.7 add_compare_fusion
  17.8 12.0 %bitcast_reduce_fusion = (f32[2,3,256]{2,1,0:T(4,128)S(1)}, f32[2,4096,256,3]{2,1,3,0:T(8,128)}) fusion(pred[4096]{0:T(1024)(128)(4,1)S(1)} %add_compare_fusion, bf16[256,2,3,256]{0,3,2,1:T(8,128)(2,1)S(1)} %bitcast.126, bf16[4096,2,256,1]{2,1,0,3:T(2,128)(2,1)} %bitcast.124), kind=kOutput, calls=%fused_computation.1 | convolution fusion | flops 3240098304 | bytes 30156800 | tf_op jit(solution)/shard_map/ngrd,cgd->grnc/dot_general | solution.py:90
  30.1 2.6 pmax.7
  32.7 11.6 %fusion.1 = f32[2,3,256]{2,1,0:T(4,128)S(1)} fusion(f32[2,4096,256,3]{2,1,3,0:T(8,128)} %get-tuple-element.8, f32[2,3,256]{2,1,0:T(4,128)S(1)} %pmax.7, pred[4096]{0:T(1024)(128)(4,1)S(1)} %add_compare_fusion), kind=kLoop, calls=%fused_computation.4 | loop fusion | flops 25164288 | bytes 25182208 | tf_op jit(solution)/shard_map/reduce_sum | solution.py:109
  44.5 0.8 copy.103
  45.3 0.7 bitcast_dynamic-update-slice_fusion.14
  47.3 0.7 bitcast_dynamic-update-slice_fusion.11
  48.7 0.7 bitcast_dynamic-update-slice_fusion.9
  49.4 0.7 bitcast_dynamic-update-slice_fusion.8
  50.1 0.7 bitcast_dynamic-update-slice_fusion.7
  50.7 0.7 bitcast_dynamic-update-slice_fusion.6
  54.1 0.7 bitcast_dynamic-update-slice_fusion.1
  55.4 0.7 fusion.34
  56.1 8.2 %all-to-all-start = ((bf16[16,2,96,384]{3,2,1,0:T(8,128)(2,1)}), bf16[16,2,96,384]{3,2,1,0:T(8,128)(2,1)S(1)}, u32[]{:S(2)}, u32[]{:S(2)}) async-start(bf16[16,2,96,384]{3,2,1,0:T(8,128)(2,1)} %fusion.34), calls=%async_computation.1 | async-start | bytes 4718592 | tf_op jit(solution)/shard_map/all_to_all | solution.py:122
  64.4 6.9 %reshape_squeeze.18 = bf16[4096,2,256]{2,1,0:T(2,128)(2,1)} reshape(bf16[1,4096,512]{2,1,0:T(8,128)(2,1)} %param.12) | data formatting | bytes 8388608 | tf_op jit(solution)/shard_map/reshape;squeeze | solution.py:84
  71.4 13.5 %fusion.3 = f32[2,3,256,256]{3,2,1,0:T(8,128)S(1)} fusion(f32[2,4096,256,3]{2,1,3,0:T(8,128)} %get-tuple-element.8, f32[2,3,256]{2,1,0:T(4,128)S(1)} %pmax.7, pred[4096]{0:T(1024)(128)(4,1)S(1)} %add_compare_fusion, bf16[4096,2,256,1]{2,1,0,3:T(2,128)(2,1)} %bitcast.125), kind=kOutput, calls=%fused_computation.6 | convolution fusion | flops 3246391296 | bytes 30943232 | tf_op jit(solution)/shard_map/grnc,cgd->ngrd/dot_general | solution.py:112
  84.8 1.6 add_bitcast_fusion
  86.5 25.5 %all-to-all-done = bf16[16,2,96,384]{3,2,1,0:T(8,128)(2,1)S(1)} async-done(((bf16[16,2,96,384]{3,2,1,0:T(8,128)(2,1)}), bf16[16,2,96,384]{3,2,1,0:T(8,128)(2,1)S(1)}, u32[]{:S(2)}, u32[]{:S(2)}) %all-to-all-start) | async-done | bytes 2359328 | tf_op jit(solution)/shard_map/all_to_all | solution.py:122
  112.0 1.7 copy.82
  113.8 1.0 reshape.60
  114.8 1.5 multiply_reduce_fusion
  116.6 0.8 multiply_convert_fusion.1
  117.6 40.8 %all_to_all.24 = bf16[16,384,96]{1,2,0:T(8,128)(2,1)} all-to-all(bf16[16,384,96]{1,2,0:T(8,128)(2,1)S(1)} %bitcast.123), channel_id=1, replica_groups=mesh['req'=16,'mlp'=2] {'req'}, dimensions={0} | all-to-all | bytes 2359296 | tf_op jit(solution)/shard_map/all_to_all | solution.py:126
  158.7 96.8 %all-gather.4.cloned.1.call-done = bf16[2048,1536]{0,1:T(8,128)(2,1)} async-done(((bf16[128,1536]{0,1:T(8,128)(2,1)}), bf16[2048,1536]{0,1:T(8,128)(2,1)}) %all-gather.4.cloned.1.call-update) | async-done | bytes 6291472 | tf_op jit(solution)/shard_map/all_gather | solution.py:136
  255.5 8.3 %fusion.9 = f32[2048,768]{1,0:T(8,128)S(1)} fusion(bf16[2048,1536]{0,1:T(8,128)(2,1)} %all-gather.4.cloned.1.call-done, bf16[2,1536,768]{2,1,0:T(8,128)(2,1)} %all-gather.6.cloned.1.call-done), kind=kOutput, calls=%fused_computation.45 | convolution fusion | flops 4831838208 | bytes 14942208 | tf_op jit(solution)/shard_map/dot_general | solution.py:137
  263.8 7.6 %multiply_convert_fusion = bf16[2048,768]{1,0:T(8,128)(2,1)} fusion(f32[2048,768]{1,0:T(8,128)S(1)} %fusion.9, bf16[2048,1536]{0,1:T(8,128)(2,1)S(1)} %copy-done.5, bf16[2,1536,768]{2,1,0:T(8,128)(2,1)S(1)} %copy-done.6), kind=kOutput, calls=%fused_computation.39 | convolution fusion | flops 4841275392 | bytes 18087936 | tf_op jit(solution)/shard_map/dot_general | solution.py:138
  271.4 9.1 %convolution_convert_fusion = bf16[2048,1536]{1,0:T(8,128)(2,1)} fusion(bf16[2048,768]{1,0:T(8,128)(2,1)} %multiply_convert_fusion, bf16[768,1536]{0,1:T(8,128)(2,1)} %all-gather.8.cloned.1.call-done), kind=kOutput, calls=%fused_computation.8 | convolution fusion | flops 4834983936 | bytes 11796480 | tf_op jit(solution)/shard_map/dot_general | solution.py:140
  280.8 143.9 %reduce-scatter.8.cloned.1.call-done = bf16[128,1536]{1,0:T(8,128)(2,1)} async-done(((bf16[2048,1536]{1,0:T(8,128)(2,1)}), bf16[128,1536]{1,0:T(8,128)(2,1)}) %reduce-scatter.8.cloned.1.call-update) | async-done | bytes 393232 | tf_op jit(solution)/shard_map/reduce_scatter | solution.py:141
  424.7 1.8 fusion.16
  (57 shorter events, 7.9 us)
Async XLA Ops:
  6.5 107.2 %reduce-scatter.10.cloned.1.call-start = ((), (), s32[]{:S(2)}) async-start(), calls=%async_computation.10 | async-start | bytes 196608
  7.9 7.0 %copy-start.3 = (bf16[1,128,512]{2,1,0:T(8,128)(2,1)S(1)}, bf16[1,128,512]{2,1,0:T(8,128)(2,1)}, u32[]{:S(2)}) copy-start(bf16[1,128,512]{2,1,0:T(8,128)(2,1)} %param.13) | copy-start | bytes 393220
  8.0 7.2 %copy-start.7 = (s32[16]{0:T(128)S(1)}, s32[16]{0:T(128)}, u32[]{:S(2)}) copy-start(s32[16]{0:T(128)} %param.16) | copy-start | bytes 196
  8.0 7.8 %copy-start.8 = (s32[16]{0:T(128)S(1)}, s32[16]{0:T(128)}, u32[]{:S(2)}) copy-start(s32[16]{0:T(128)} %param.15) | copy-start | bytes 196
  32.7 12.6 %copy-start = (bf16[96,6144]{1,0:T(8,128)(2,1)S(1)}, bf16[96,6144]{1,0:T(8,128)(2,1)}, u32[]{:S(2)}) copy-start(bf16[96,6144]{1,0:T(8,128)(2,1)} %param.18) | copy-start | bytes 3538948
  32.7 12.6 %copy-start.1 = (bf16[96,6144]{1,0:T(8,128)(2,1)S(1)}, bf16[96,6144]{1,0:T(8,128)(2,1)}, u32[]{:S(2)}) copy-start(bf16[96,6144]{1,0:T(8,128)(2,1)} %param.17) | copy-start | bytes 3538948
  56.1 55.8 %all-to-all-start = ((bf16[16,2,96,384]{3,2,1,0:T(8,128)(2,1)}), bf16[16,2,96,384]{3,2,1,0:T(8,128)(2,1)S(1)}, u32[]{:S(2)}, u32[]{:S(2)}) async-start(bf16[16,2,96,384]{3,2,1,0:T(8,128)(2,1)} %fusion.34), calls=%async_computation.1 | async-start | bytes 4718592 | tf_op jit(solution)/shard_map/all_to_all | solution.py:122
  64.3 7.0 %copy-start.4 = (bf16[1,128,512]{2,1,0:T(8,128)(2,1)S(1)}, bf16[1,128,512]{2,1,0:T(8,128)(2,1)}, u32[]{:S(2)}) copy-start(bf16[1,128,512]{2,1,0:T(8,128)(2,1)} %param.14) | copy-start | bytes 393220
  64.3 50.5 %reduce-scatter.6.cloned.1.call-start = ((), (), s32[]{:S(2)}) async-start(), calls=%async_computation.5 | async-start | bytes 2359296 | tf_op jit(solution)/shard_map/reduce_scatter | solution.py:129
  86.4 72.3 %all-gather.6.cloned.1.call-start = ((), (), s32[]{:S(2)}) async-start(), calls=%async_computation.7 | async-start | bytes 7077888 | tf_op jit(solution)/shard_map/all_gather | solution.py:125
  113.7 141.7 %all-gather.4.cloned.1.call-start = ((), (), s32[]{:S(2)}) async-start(), calls=%async_computation.6 | async-start | bytes 6684672 | tf_op jit(solution)/shard_map/all_gather | solution.py:136
  114.8 2.7 copy-start.2
  117.5 153.9 %all-gather.8.cloned.1.call-start = ((), (), s32[]{:S(2)}) async-start(), calls=%async_computation.8 | async-start | bytes 3538944 | tf_op jit(solution)/shard_map/all_gather | solution.py:127
  158.4 266.3 %reduce-scatter.8.cloned.1.call-start = ((), (), s32[]{:S(2)}) async-start(), calls=%async_computation.9 | async-start | bytes 6684672 | tf_op jit(solution)/shard_map/reduce_scatter | solution.py:141
  255.5 8.3 %copy-start.5 = (bf16[2048,1536]{0,1:T(8,128)(2,1)S(1)}, bf16[2048,1536]{0,1:T(8,128)(2,1)}, u32[]{:S(2)}) copy-start(bf16[2048,1536]{0,1:T(8,128)(2,1)} %all-gather.4.cloned.1.call-done) | copy-start | bytes 18874372
  255.5 8.3 %copy-start.6 = (bf16[2,1536,768]{2,1,0:T(8,128)(2,1)S(1)}, bf16[2,1536,768]{2,1,0:T(8,128)(2,1)}, u32[]{:S(2)}) copy-start(bf16[2,1536,768]{2,1,0:T(8,128)(2,1)} %all-gather.6.cloned.1.call-done) | copy-start | bytes 14155780
Sparse Core Ops, SparseCore 0:
  45.4 10.0 reduce-scatter.9
  86.6 10.3 reduce-scatter.5
  113.8 20.2 all-gather.5
  137.1 118.3 all-gather.3
  256.9 9.0 all-gather.7
  280.7 143.9 reduce-scatter.7
